TPU v7x, 32 devices: a whole 2x2x4 slice. The times are simulated.
32 devices in a mesh: seq: 8 (over z, x), head: 4 (over y, core).
Axes of the slice: x: 2, y: 2, z: 4, core: 2. Of those that a mesh axis runs over, the one named last changes fastest.
Arguments:
- block_input: bfloat16 [4096, 1024], P('seq'), may hold values from -6 to 6
- norm1_gain: float32 [1024], replicated, may hold values from 0.5 to 1.5
- w_in: bfloat16 [1024, 8, 768], P(None, 'head'), may hold values from -0.1875 to 0.1875
- w_ba: bfloat16 [1024, 2, 8], P(None, None, 'head'), may hold values from -0.1875 to 0.1875
- conv_weight: float32 [512, 8, 4], P(None, 'head'), may hold values from -2.5 to 2.5
- decay_log: float32 [8], P('head'), may hold values from -9 to -3.5
- gnorm_gain: float32 [256], replicated, may hold values from 0.5 to 1.5
- w_out: bfloat16 [256, 8, 1024], P(None, 'head'), may hold values from -0.1875 to 0.1875
- norm2_gain: float32 [1024], replicated, may hold values from 0.5 to 1.5
- w_up: bfloat16 [1024, 2, 2816], P(None, None, 'head'), may hold values from -0.1875 to 0.1875
- w_down: bfloat16 [1024, 2816], P(None, 'head'), may hold values from -0.15625 to 0.15625
- grad_out: bfloat16 [4096, 1024], P('seq'), may hold values from -6 to 6
Outputs:
- result: float32 [4096, 1024], P('seq')
- input_grad: float32 [4096, 1024], P('seq')
- norm1_gain_grad: float32 [1024], replicated
- input_weight_gradient: float32 [1024, 8, 768], P('seq', 'head')
- w_ba_grad: float32 [1024, 2, 8], P('seq', None, 'head')
- conv_grad: float32 [512, 8, 4], P('seq', 'head')
- log_decay_gradient: float32 [8], P('head')
- gnorm_gain_grad: float32 [256], replicated
- w_out_grad: float32 [256, 8, 1024], P('seq', 'head')
- norm2_gain_grad: float32 [1024], replicated
- w_up_grad: float32 [1024, 2, 2816], P('seq', None, 'head')
- w_down_grad: float32 [1024, 2816], P('seq', 'head')
All inputs are finite; a program needn't handle non-finite values.
Results may differ from a plain program's by a relative error of at most 0.025.
The roundings to bfloat16 on the way count: a program that leaves them out, or rounds other values in their place, can miss the bound.
Values may be sent and summed in bfloat16 or wider, within the bound.
A program may use at most 128 MiB of HBM per device.

v0:
```python
import jax
import jax.numpy as jnp
from jax import lax
from jax.sharding import PartitionSpec as P

DK = 128
DV = 256
CONV = 4
STRETCH = 64


EPSILON = 1e-06
NEGATIVE = -1e30
MATMUL_ACCURACY = lax.Precision.HIGHEST


def shifted(block, axis, distance):
    devices = range(lax.axis_size(axis))
    route = [(i - distance, i) for i in devices if i - distance in devices]
    return lax.ppermute(block, axis, route)


def prefix_2(part, axis, combine, identity, reverse):
    count = lax.axis_size(axis)
    place = lax.axis_index(axis)
    ahead = count - 1 - place if reverse else place
    gathered = jax.tree.map(lambda a: lax.all_gather(a, axis), part)
    state = jax.tree.map(lambda a, e: jnp.zeros_like(a) + jnp.asarray(e, a.dtype), part, identity)

    def one(lap, state):
        source = count - 1 - lap if reverse else lap
        return combine(
            state, jax.tree.map(lambda a: lax.dynamic_index_in_dim(a, source, 0, False), gathered)
        )

    return lax.fori_loop(0, ahead, one, state)


def dot_high(left, right):
    return jnp.dot(left, right, precision=MATMUL_ACCURACY)


def rms_apply(values, gain):
    return values * lax.rsqrt(jnp.mean(values * values, axis=-1, keepdims=True) + EPSILON) * gain


def features(edged, mixer_in, conv_weight, decay_log):
    length = edged.shape[0] - (CONV - 1)
    mixed = edged[0:length] * conv_weight[:, :, 0].T
    for index in range(1, CONV):
        mixed = mixed + edged[index : index + length] * conv_weight[:, :, index].T
    active = jax.nn.silu(mixed)
    query = active[..., :DK]
    key = active[..., DK : 2 * DK]
    value = active[..., 2 * DK :]
    query = (
        query * lax.rsqrt(jnp.sum(query * query, axis=-1, keepdims=True) + EPSILON) * DK ** (-0.5)
    )
    key = key * lax.rsqrt(jnp.sum(key * key, axis=-1, keepdims=True) + EPSILON)
    beta = jax.nn.sigmoid(mixer_in[:, 0])
    logdecay = -jnp.exp(decay_log) * jax.nn.softplus(mixer_in[:, 1])
    return (query, key, value, beta, logdecay)


def stretch_terms(query, key, value, beta, logdecay):
    width = query.shape[0]
    cumul = jnp.cumsum(logdecay)
    spread = cumul[:, None] - cumul[None, :]
    row_pos = lax.broadcasted_iota(jnp.int32, (width, width), 0)
    column = lax.broadcasted_iota(jnp.int32, (width, width), 1)
    strict = jnp.exp(jnp.where(row_pos > column, spread, NEGATIVE))
    inclusive = jnp.exp(jnp.where(row_pos >= column, spread, NEGATIVE))
    lower = beta[:, None] * strict * dot_high(key, key.T)
    system = jnp.eye(width, dtype=query.dtype) + lower
    solved_value = jax.scipy.linalg.solve_triangular(
        system, beta[:, None] * value, lower=True, unit_diagonal=True
    )
    solved_key = jax.scipy.linalg.solve_triangular(
        system, (beta * jnp.exp(cumul))[:, None] * key, lower=True, unit_diagonal=True
    )
    scores = inclusive * dot_high(query, key.T)
    query_map = jnp.exp(cumul)[:, None] * query - dot_high(scores, solved_key)
    out_fixed = dot_high(scores, solved_value)
    key_end = jnp.exp(cumul[-1] - cumul)[:, None] * key
    transit = jnp.exp(cumul[-1]) * jnp.eye(key.shape[1], dtype=query.dtype) - dot_high(
        key_end.T, solved_key
    )
    feed = dot_high(key_end.T, solved_value)
    return (query_map, out_fixed, transit, feed)


def stretch_head(query, key, value, beta, logdecay):
    count = query.shape[0] // STRETCH

    def split(array):
        return array.reshape((count, STRETCH) + array.shape[1:])

    return jax.vmap(stretch_terms)(
        split(query), split(key), split(value), split(beta), split(logdecay)
    )


def stretch_heads(query, key, value, beta, logdecay):
    return jax.vmap(stretch_head, in_axes=1, out_axes=0)(query, key, value, beta, logdecay)


def scan_head(terms, state):

    def scan_advance(carry, parts):
        query_map, out_fixed, transit, feed = parts
        return (dot_high(transit, carry) + feed, dot_high(query_map, carry) + out_fixed)

    final, layer_outputs = lax.scan(scan_advance, state, terms)
    return (layer_outputs.reshape(-1, state.shape[1]), final)


def scan_heads(terms, state):
    return jax.vmap(scan_head, in_axes=(0, 0), out_axes=(1, 0))(terms, state)


def affine_head(terms):
    start = (jnp.eye(DK, dtype=jnp.float32), jnp.zeros((DK, DV), jnp.float32))

    def affine_advance(carry, parts):
        product, state = carry
        part_map, part_fixed, part_transit, part_feed = parts
        moved = (dot_high(part_transit, product), dot_high(part_transit, state) + part_feed)
        return (moved, (dot_high(part_map, product), dot_high(part_map, state) + part_fixed))

    (product, state), (effective_query, local_out) = lax.scan(affine_advance, start, terms)
    return (product, state, effective_query.reshape(-1, DK), local_out.reshape(-1, DV))


def affine_heads(terms):
    return jax.vmap(affine_head, in_axes=0, out_axes=(0, 0, 1, 1))(terms)


def combine_maps(earlier, later):
    product = jnp.einsum("hij,hjk->hik", later[0], earlier[0], precision=MATMUL_ACCURACY)
    state = jnp.einsum("hij,hjk->hik", later[0], earlier[1], precision=MATMUL_ACCURACY) + later[1]
    return (product, state)


def gated(layer_outputs, gate, gain):
    return rms_apply(layer_outputs, gain) * jax.nn.silu(gate)


def swiglu(gate_up):
    return jax.nn.silu(gate_up[:, 0]) * gate_up[:, 1]


def shards(
    block_input,
    norm1_gain,
    w_in,
    w_ba,
    conv_weight,
    decay_log,
    gnorm_gain,
    w_out,
    norm2_gain,
    w_up,
    w_down,
    grad_out,
):
    length = block_input.shape[0]
    heads = w_in.shape[1]
    channels = conv_weight.shape[0]
    identity = (
        jnp.broadcast_to(jnp.eye(DK, dtype=jnp.float32), (heads, DK, DK)),
        jnp.zeros((heads, DK, DV), jnp.float32),
    )
    tokens_wide = block_input.astype(jnp.float32)
    normed, pull_first = jax.vjp(rms_apply, tokens_wide, norm1_gain)
    normed_b = normed.astype(jnp.bfloat16)
    projected = jnp.einsum(
        "td,dhc->thc", normed_b, w_in, preferred_element_type=jnp.float32
    ).astype(jnp.bfloat16)
    mixer_in = jnp.einsum("td,dch->tch", normed_b, w_ba, preferred_element_type=jnp.float32)
    edge = shifted(projected[length - (CONV - 1) :, :, :channels], "seq", 1)
    edged = jnp.concatenate([edge, projected[:, :, :channels]], 0).astype(jnp.float32)
    feats, pull_feat = jax.vjp(features, edged, mixer_in, conv_weight, decay_log)
    terms, pull_terms = jax.vjp(stretch_heads, *feats)
    transit_all, local_state, effective_query, local_out = affine_heads(terms)
    prefix = prefix_2((transit_all, local_state), "seq", combine_maps, identity, False)
    carried = prefix[1]
    (layer_outputs, final), pull_scan = jax.vjp(scan_heads, terms, carried)
    gate_wide = projected[:, :, channels:].astype(jnp.float32)
    gated_out, pull_gate = jax.vjp(gated, layer_outputs, gate_wide, gnorm_gain)
    gated_b = gated_out.astype(jnp.bfloat16)
    mixer_part = jnp.einsum("thc,chd->td", gated_b, w_out, preferred_element_type=jnp.float32)
    mixed = lax.psum(mixer_part.astype(jnp.bfloat16), "head").astype(jnp.float32)
    hidden = tokens_wide + mixed
    hidden_n, pull_second = jax.vjp(rms_apply, hidden, norm2_gain)
    hidden_b = hidden_n.astype(jnp.bfloat16)
    gate_up = jnp.einsum("td,dcf->tcf", hidden_b, w_up, preferred_element_type=jnp.float32)
    swish, pull_swish = jax.vjp(swiglu, gate_up)
    swish_b = swish.astype(jnp.bfloat16)
    ffn_part = lax.dot_general(
        swish_b, w_down, (((1,), (1,)), ((), ())), preferred_element_type=jnp.float32
    )
    ffn_total = lax.psum(ffn_part.astype(jnp.bfloat16), "head").astype(jnp.float32)
    result = hidden + ffn_total
    act_grad = jnp.dot(grad_out, w_down, preferred_element_type=jnp.float32)
    down_grad = lax.dot_general(
        grad_out, swish_b, (((0,), (0,)), ((), ())), preferred_element_type=jnp.float32
    )
    (gate_up_grad,) = pull_swish(act_grad)
    gate_up_b = gate_up_grad.astype(jnp.bfloat16)
    up_grad = jnp.einsum("td,tcf->dcf", hidden_b, gate_up_b, preferred_element_type=jnp.float32)
    second_part = jnp.einsum("tcf,dcf->td", gate_up_b, w_up, preferred_element_type=jnp.float32)
    second_total = lax.psum(second_part, "head")
    hidden_grad, gain_second = pull_second(second_total)
    stream = grad_out.astype(jnp.float32) + hidden_grad
    stream_b = stream.astype(jnp.bfloat16)
    out_weight_grad = jnp.einsum(
        "thc,td->chd", gated_b, stream_b, preferred_element_type=jnp.float32
    )
    gated_grad = jnp.einsum("td,chd->thc", stream_b, w_out, preferred_element_type=jnp.float32)
    output_gradient, gate_grad, gain_gated = pull_gate(gated_grad)
    cross_product = jnp.einsum(
        "blr,blc->lrc", effective_query, output_gradient, precision=MATMUL_ACCURACY
    )
    suffix = prefix_2(
        (jnp.swapaxes(transit_all, 1, 2), cross_product), "seq", combine_maps, identity, True
    )
    later_grad = suffix[1]
    term_grad, carried_grad = pull_scan((output_gradient, later_grad))
    feat_grad = pull_terms(term_grad)
    edged_grad, mixer_grad, conv_grad, log_decay_gradient = pull_feat(tuple(feat_grad))
    back_edge = shifted(edged_grad[: CONV - 1], "seq", -1)
    channel_grad = edged_grad[CONV - 1 :]
    channel_grad = jnp.concatenate(
        [channel_grad[: length - (CONV - 1)], channel_grad[length - (CONV - 1) :] + back_edge], 0
    )
    proj_grad = jnp.concatenate([channel_grad, gate_grad], 2).astype(jnp.bfloat16)
    mixer_b = mixer_grad.astype(jnp.bfloat16)
    in_weight_grad = jnp.einsum(
        "td,thc->dhc", normed_b, proj_grad, preferred_element_type=jnp.float32
    )
    gate_weight_grad = jnp.einsum(
        "td,tch->dch", normed_b, mixer_b, preferred_element_type=jnp.float32
    )
    first_part = jnp.einsum("thc,dhc->td", proj_grad, w_in, preferred_element_type=jnp.float32)
    first_part = first_part + jnp.einsum(
        "tch,dch->td", mixer_b, w_ba, preferred_element_type=jnp.float32
    )
    first_total, gated_total = lax.psum((first_part, gain_gated), "head")
    input_part, gain_first = pull_first(first_total)
    input_grad = stream + input_part
    gain_one, gain_two, gain_norm, decay_total = lax.psum(
        (gain_first, gain_second, gated_total, log_decay_gradient), "seq"
    )
    in_share, gate_share, conv_share, out_share, up_share, down_share = (
        lax.psum_scatter(in_weight_grad, "seq", scatter_dimension=0, tiled=True),
        lax.psum_scatter(gate_weight_grad, "seq", scatter_dimension=0, tiled=True),
        lax.psum_scatter(conv_grad, "seq", scatter_dimension=0, tiled=True),
        lax.psum_scatter(out_weight_grad, "seq", scatter_dimension=0, tiled=True),
        lax.psum_scatter(up_grad, "seq", scatter_dimension=0, tiled=True),
        lax.psum_scatter(down_grad, "seq", scatter_dimension=0, tiled=True),
    )
    return (
        result,
        input_grad,
        gain_one,
        in_share,
        gate_share,
        conv_share,
        decay_total,
        gain_norm,
        out_share,
        gain_two,
        up_share,
        down_share,
    )


def solution(mesh):
    return jax.shard_map(
        shards,
        mesh=mesh,
        in_specs=(
            P("seq", None),
            P(),
            P(None, "head", None),
            P(None, None, "head"),
            P(None, "head", None),
            P("head"),
            P(),
            P(None, "head", None),
            P(),
            P(None, None, "head"),
            P(None, "head"),
            P("seq", None),
        ),
        out_specs=(
            P("seq", None),
            P("seq", None),
            P(),
            P("seq", "head", None),
            P("seq", None, "head"),
            P("seq", "head", None),
            P("head"),
            P(),
            P("seq", "head", None),
            P(),
            P("seq", None, "head"),
            P("seq", "head"),
        ),
        check_vma=False,
    )
```

profile of v0, /device:TPU:0, one launch (start us, length us, event | category | flops | bytes accessed | tf_op | source)
XLA Modules:
  0.0 1185.9 jit_solution(14367459867563297318)
XLA Ops:
  13.4 5.4 collective-permute-start
  36.3 80.2 %custom-call.16 = f32[2,8,1,64,64]{3,4,2,1,0:T(8,128)} custom-call(f32[2,8,1,64,64]{4,3,2,1,0:T(8,128)} %fusion.116), custom_call_target="InvertDiagBlocksLowerTriangular" | custom-call | tf_op jit(solution)/shard_map/jvp(vmap(vmap(jit(_solve_triangular))))/triangular_solve | solution.py:78
  131.6 34.9 %while.81 = (s32[]{:T(128)}, f32[2,128,128]{2,1,0:T(8,128)S(1)}, f32[2,128,256]{2,1,0:T(8,128)S(1)}, f32[8,2,64,128]{3,2,0,1:T(8,128)}, f32[8,2,128,128]{3,2,1,0...) while((s32[]{:T(128)}, f32[2,128,128]{2,1,0:T(8,128)S(1)}, ...), condition=%wide.region_5.6_spmd.clone, body=%wide.region_4.5_spmd.clone.sunk | while | flops 176291840 | bytes 2361959 | solution.py:130
  171.5 35.9 %all-gather.9.cloned.1.call-done = f32[16,128,128]{2,1,0:T(8,128)} async-done(((f32[2,128,128]{2,1,0:T(8,128)}), f32[16,128,128]{2,1,0:T(8,128)}) %all-gather.9.cloned.1.call-update) | async-done | bytes 1048592 | tf_op jit(solution)/shard_map/all_gather | solution.py:27
  207.4 50.5 %all-gather.11.cloned.1.call-done = f32[16,128,256]{2,1,0:T(8,128)} async-done(((f32[2,128,256]{2,1,0:T(8,128)}), f32[16,128,256]{2,1,0:T(8,128)}) %all-gather.11.cloned.1.call-update) | async-done | bytes 2097168 | tf_op jit(solution)/shard_map/all_gather | solution.py:27
  260.6 32.5 %while.78 = (s32[]{:T(128)}, f32[2,128,256]{2,1,0:T(8,128)S(1)}, f32[8,2,64,256]{3,2,1,0:T(8,128)}, f32[8,2,128,256]{3,2,1,0:T(8,128)}, f32[8,2,128,128]{3,2,1,0...) while((s32[]{:T(128)}, f32[2,128,256]{2,1,0:T(8,128)S(1)}, ...), condition=%wide.region_9.10_spmd, body=%wide.region_8.9_spmd.sunk | while | flops 151093248 | bytes 2558557 | solution.py:113
  299.6 45.1 %all-reduce.25.cloned.1.call-done = bf16[512,1024]{1,0:T(8,128)(2,1)} async-done(((bf16[512,1024]{1,0:T(8,128)(2,1)}), bf16[512,1024]{1,0:T(8,128)(2,1)}) %all-reduce.25.cloned.1.call-update) | async-done | bytes 1048592 | tf_op jit(solution)/shard_map/psum | solution.py:192
  363.0 46.9 %all-reduce.29.cloned.1.call-done = f32[512,1024]{1,0:T(8,128)} async-done(((f32[512,1024]{1,0:T(8,128)}), f32[512,1024]{1,0:T(8,128)}) %all-reduce.29.cloned.1.call-update) | async-done | bytes 2097168 | tf_op jit(solution)/shard_map/psum | solution.py:212
  413.4 35.1 %all-reduce.27.cloned.1.call-done = bf16[512,1024]{1,0:T(8,128)(2,1)} async-done(((bf16[512,1024]{1,0:T(8,128)(2,1)}), bf16[512,1024]{1,0:T(8,128)(2,1)}) %all-reduce.27.cloned.1.call-update) | async-done | bytes 1048592 | tf_op jit(solution)/shard_map/psum | solution.py:202
  469.8 22.1 %all-gather.13.cloned.1.call-done = f32[16,128,128]{2,1,0:T(8,128)} async-done(((f32[2,128,128]{2,1,0:T(8,128)}), f32[16,128,128]{2,1,0:T(8,128)}) %all-gather.13.cloned.1.call-update) | async-done | bytes 1048592 | tf_op jit(solution)/shard_map/all_gather | solution.py:27
  491.9 50.5 %all-gather.15.cloned.1.call-done = f32[16,128,256]{2,1,0:T(8,128)} async-done(((f32[2,128,256]{2,1,0:T(8,128)}), f32[16,128,256]{2,1,0:T(8,128)}) %all-gather.15.cloned.1.call-update) | async-done | bytes 2097168 | tf_op jit(solution)/shard_map/all_gather | solution.py:27
  542.4 10.2 while.79
  557.3 72.8 %while.80 = (s32[]{:T(128)}, f32[2,128,256]{2,1,0:T(8,128)S(1)}, f32[8,2,64,128]{3,2,0,1:T(8,128)}, f32[8,2,64,256]{3,2,1,0:T(8,128)}, f32[8,2,128,128]{2,3,1,0:...) while((s32[]{:T(128)}, f32[2,128,256]{2,1,0:T(8,128)S(1)}, ...), condition=%wide.region_20.21_spmd, body=%wide.region_19.20_spmd.sunk | while | flops 302055424 | bytes 3804813 | solution.py:113
  687.8 5.6 pad_add_fusion
  702.1 6.3 fusion.106
  712.5 6.7 fusion.175
  721.2 5.8 psum.69
  728.7 18.9 %reduce-scatter.18.cloned.1.call-done = f32[64,8]{1,0:T(8,128)} async-done(((f32[512,8]{1,0:T(8,128)}), f32[64,8]{1,0:T(8,128)}) %reduce-scatter.18.cloned.1.call-update) | async-done | bytes 2064
  749.2 63.8 %reduce-scatter.16.cloned.1.call-done = f32[128,4]{1,0:T(8,128)} async-done(((f32[1024,4]{1,0:T(8,128)}), f32[128,4]{1,0:T(8,128)}) %reduce-scatter.16.cloned.1.call-update) | async-done | bytes 2064
  814.5 51.9 %all-reduce.31.cloned.1.call-done = f32[512,1024]{1,0:T(8,128)} async-done(((f32[512,1024]{1,0:T(8,128)}), f32[512,1024]{1,0:T(8,128)}) %all-reduce.31.cloned.1.call-update) | async-done | bytes 2097168 | tf_op jit(solution)/shard_map/psum | solution.py:248
  869.0 23.7 %all-reduce.18 = (f32[1024]{0:T(1024)}, f32[2]{0:T(128)}, f32[256]{0:T(256)}, f32[1024]{0:T(1024)}) all-reduce(f32[1024]{0:T(1024)S(1)} %get-tuple-element.588, f32[2]{0:T(128)S(1)} %negate_multiply_fusion, f32[256]{0:T(256)S(1)} %psum.69, f32[1024]{0:T(1024)S(1)} %copy-done.89), channel_id=1, replica_groups=mesh['seq'=8,'head'=4] {'seq'}, use_global_device_ids=true, to_apply=%region_36.38 | all-reduce | flops 2306 | bytes 18448 | tf_op jit(solution)/shard_map/psum | solution.py:251
  897.2 91.1 %reduce-scatter.10.cloned.1.call-done = f32[128,2,768]{2,0,1:T(8,128)} async-done(((f32[1024,2,768]{2,0,1:T(8,128)}), f32[128,2,768]{2,0,1:T(8,128)}) %reduce-scatter.10.cloned.1.call-update) | async-done | bytes 786448 | tf_op jit(solution)/shard_map/reduce_scatter | solution.py:255
  990.9 73.6 %reduce-scatter.14.cloned.1.call-done = f32[128,704]{0,1:T(8,128)} async-done(((f32[1024,704]{0,1:T(8,128)}), f32[128,704]{0,1:T(8,128)}) %reduce-scatter.14.cloned.1.call-update) | async-done | bytes 360464 | tf_op jit(solution)/shard_map/reduce_scatter | solution.py:260
  1064.5 114.4 %reduce-scatter.12.cloned.1.call-done = f32[128,2,704]{0,2,1:T(8,128)} async-done(((f32[1024,2,704]{0,2,1:T(8,128)}), f32[128,2,704]{0,2,1:T(8,128)}) %reduce-scatter.12.cloned.1.call-update) | async-done | bytes 720912 | tf_op jit(solution)/shard_map/reduce_scatter | solution.py:259
  (520 shorter events, 334.2 us)
Async XLA Ops:
  7.2 200.2 %all-gather.9.cloned.1.call-start = ((), (), s32[]{:S(2)}) async-start(), calls=%async_computation.12 | async-start | bytes 1179648 | tf_op jit(solution)/shard_map/all_gather | solution.py:27
  13.4 12.8 %collective-permute-start = (bf16[3,2,512]{2,0,1:T(4,128)(2,1)}, bf16[3,2,512]{2,0,1:T(4,128)(2,1)}, u32[]{:S(2)}, u32[]{:S(2)}) collective-permute-start(bf16[3,2,512]{2,0,1:T(4,128)(2,1)} %slice.121), channel_id=1, source_target_pairs={{0,4},{4,8},{8,12},{12,16},{16,20},{20,24},{24,28},{1,5},{5,9},{9,... | collective-permute-start | bytes 18440 | tf_op jit(solution)/shard_map/ppermute | solution.py:20
  18.9 107.7 %copy-start.49 = (f32[128,128]{1,0:T(8,128)}, f32[128,128]{1,0:T(8,128)S(1)}, u32[]{:S(2)}) copy-start(f32[128,128]{1,0:T(8,128)S(1)} %fusion.180) | copy-start | bytes 196612
  20.9 14.3 %copy-start.60 = (pred[64,64]{1,0:T(8,128)(4,1)}, pred[64,64]{1,0:T(8,128)(4,1)S(1)}, u32[]{:S(2)}) copy-start(pred[64,64]{1,0:T(8,128)(4,1)S(1)} %get-tuple-element.716) | copy-start | bytes 12292
  22.7 104.0 %copy-start.55 = (f32[2,8,64]{2,1,0:T(8,128)}, f32[2,8,64]{2,1,0:T(8,128)S(1)}, u32[]{:S(2)}) copy-start(f32[2,8,64]{2,1,0:T(8,128)S(1)} %get-tuple-element.706) | copy-start | bytes 12292
  23.9 97.4 %copy-start.53 = (pred[64,64]{1,0:T(8,128)(4,1)}, pred[64,64]{1,0:T(8,128)(4,1)S(1)}, u32[]{:S(2)}) copy-start(pred[64,64]{1,0:T(8,128)(4,1)S(1)} %get-tuple-element.718) | copy-start | bytes 12292
  167.2 90.7 %all-gather.11.cloned.1.call-start = ((), (), s32[]{:S(2)}) async-start(), calls=%async_computation.13 | async-start | bytes 2359296 | tf_op jit(solution)/shard_map/all_gather | solution.py:27
  167.9 176.7 %all-reduce.25.cloned.1.call-start = ((), (), s32[]{:S(2)}) async-start(), calls=%async_computation.5 | async-start | bytes 2097152 | tf_op jit(solution)/shard_map/psum | solution.py:192
  299.5 47.3 %copy-start.74 = (f32[1024]{0:T(1024)S(1)}, f32[1024]{0:T(1024)}, u32[]{:S(2)}) copy-start(f32[1024]{0:T(1024)} %param.32) | copy-start | bytes 12292
  299.5 110.4 %all-reduce.29.cloned.1.call-start = ((), (), s32[]{:S(2)}) async-start(), calls=%async_computation.7 | async-start | bytes 4194304 | tf_op jit(solution)/shard_map/psum | solution.py:212
  357.9 90.6 %all-reduce.27.cloned.1.call-start = ((), (), s32[]{:S(2)}) async-start(), calls=%async_computation.6 | async-start | bytes 2097152 | tf_op jit(solution)/shard_map/psum | solution.py:202
  361.6 130.3 %all-gather.13.cloned.1.call-start = ((), (), s32[]{:S(2)}) async-start(), calls=%async_computation.14 | async-start | bytes 1179648 | tf_op jit(solution)/shard_map/all_gather | solution.py:27
  362.4 179.9 %all-gather.15.cloned.1.call-start = ((), (), s32[]{:S(2)}) async-start(), calls=%async_computation.15 | async-start | bytes 2359296 | tf_op jit(solution)/shard_map/all_gather | solution.py:27
  459.8 267.2 %all-reduce.33.cloned.1.call-start = ((), (), s32[]{:S(2)}) async-start(), calls=%async_computation.18 | async-start | bytes 4194304
  469.7 277.9 %reduce-scatter.18.cloned.1.call-start = ((), (), s32[]{:S(2)}) async-start(), calls=%async_computation.17 | async-start | bytes 294912
  557.3 72.8 %copy-start.56 = (f32[2,8,64]{2,1,0:T(8,128)S(1)}, f32[2,8,64]{2,1,0:T(8,128)}, u32[]{:S(2)}) copy-start(f32[2,8,64]{2,1,0:T(8,128)} %copy-done.55) | copy-start | bytes 12292
  684.6 12.4 %collective-permute-start.1 = (f32[3,2,512]{2,0,1:T(4,128)S(1)}, f32[3,2,512]{2,0,1:T(4,128)S(1)}, u32[]{:S(2)}, u32[]{:S(2)}) collective-permute-start(f32[3,2,512]{2,0,1:T(4,128)S(1)} %pad_add_fusion.1), channel_id=1, source_target_pairs={{4,0},{8,4},{12,8},{16,12},{20,16},{24,20},{28,24},{5,1},{9,5},{13... | collective-permute-start | bytes 36872 | tf_op jit(solution)/shard_map/ppermute | solution.py:20
  685.9 127.1 %reduce-scatter.16.cloned.1.call-start = ((), (), s32[]{:S(2)}) async-start(), calls=%async_computation.16 | async-start | bytes 589824
  696.9 169.5 %all-reduce.31.cloned.1.call-start = ((), (), s32[]{:S(2)}) async-start(), calls=%async_computation.8 | async-start | bytes 4194304 | tf_op jit(solution)/shard_map/psum | solution.py:248
  702.0 286.3 %reduce-scatter.10.cloned.1.call-start = ((), (), s32[]{:S(2)}) async-start(), calls=%async_computation.9 | async-start | bytes 7077888 | tf_op jit(solution)/shard_map/reduce_scatter | solution.py:255
  708.4 356.1 %reduce-scatter.14.cloned.1.call-start = ((), (), s32[]{:S(2)}) async-start(), calls=%async_computation.11 | async-start | bytes 3244032 | tf_op jit(solution)/shard_map/reduce_scatter | solution.py:260
  712.5 466.4 %reduce-scatter.12.cloned.1.call-start = ((), (), s32[]{:S(2)}) async-start(), calls=%async_computation.10 | async-start | bytes 6488064 | tf_op jit(solution)/shard_map/reduce_scatter | solution.py:259
  719.3 149.7 %copy-start.89 = (f32[1024]{0:T(1024)S(1)}, f32[1024]{0:T(1024)}, u32[]{:S(2)}) copy-start(f32[1024]{0:T(1024)} %get-tuple-element.584) | copy-start | bytes 12292
  719.3 173.4 %copy-start.86 = (f32[512]{0:T(512)S(1)}, f32[512]{0:T(512)}, u32[]{:S(2)}) copy-start(f32[512]{0:T(512)} %copy-done.85) | copy-start | bytes 6148
  (97 other events, 331.0 us)
Sparse Core Ops, SparseCore 0:
  167.3 40.0 all-gather.8
  210.0 47.7 all-gather.10
  299.7 44.9 all-reduce.24
  358.0 51.8 all-reduce.28
  412.1 36.3 all-reduce.26
  451.1 40.7 all-gather.12
  494.6 47.7 all-gather.14
  546.0 100.9 all-reduce.32
  686.0 61.5 reduce-scatter.17
  751.4 61.5 reduce-scatter.15
  816.0 50.3 all-reduce.30
  869.8 118.4 reduce-scatter.9
  992.4 72.0 reduce-scatter.13
  1068.6 110.2 reduce-scatter.11
where the time goes:
time: 1190 us
  waiting for transfers between devices  701 us (59%)
  matrix products  218 us (18%)
  other arithmetic  130 us (11%)
  local copies, waits for them, and re-layouts  81.8 us (7%)
  blocking collectives  29.5 us (2%)
  between operations  16.6 us (1%)
    all_gather x4, waiting for transfers between devices, prefix_2(): gathered = jax.tree.map(lambda a: lax.all_gather(a, axis), part)  159 us
    dot_general x90, matrix products, dot_high(): return jnp.dot(left, right, precision=MATMUL_ACCURACY)  150 us
    reduce_scatter x1, waiting for transfers between devices, shards(): lax.psum_scatter(up_grad, 'seq', scatter_dimension=0, tiled=True)  114 us
    reduce_scatter x1, waiting for transfers between devices, shards(): lax.psum_scatter(in_weight_grad, 'seq', scatter_dimension=0, tiled=True)  91.1 us
    unnamed x17, waiting for transfers between devices  83.7 us
    another operation x5, other arithmetic, stretch_terms(): jax.scipy.linalg.solve_triangular(system, (beta * jnp.exp(cumul))[:, None...  82 us
    reduce_scatter x1, waiting for transfers between devices, shards(): lax.psum_scatter(down_grad, 'seq', scatter_dimension=0, tiled=True)  73.6 us
    psum x1, waiting for transfers between devices, shards(): first_total, gated_total = lax.psum((first_part, gain_gated), 'head')  51.9 us
  transfers between devices with their start and end apart: 16, of which 13 were waited for; matrix products, arithmetic and copies ran while one was open for 19% of the time, Pallas kernels for 0%

commit v1 on v0

v1 whole, which is shorter than its diff:
```python
import jax
import jax.numpy as jnp
from jax import lax
from jax.sharding import PartitionSpec as P

DK = 128
DV = 256
CONV = 4
STRETCH = 64


EPSILON = 1e-06
NEGATIVE = -1e30
FINE = lax.Precision.HIGH


def shifted(block, axis, distance):
    devices = range(lax.axis_size(axis))
    route = [(i - distance, i) for i in devices if i - distance in devices]
    return lax.ppermute(block, axis, route)


def head_sum(part):
    return lax.psum(part.astype(jnp.bfloat16), "head")


def seq_share(grad):
    return lax.psum_scatter(
        grad.astype(jnp.bfloat16), "seq", scatter_dimension=0, tiled=True
    ).astype(jnp.float32)


def carried_states(part, reverse):
    count = lax.axis_size("seq")
    place = lax.axis_index("seq")
    gathered = lax.all_gather(part.astype(jnp.bfloat16), "seq")
    order = range(count - 1, 0, -1) if reverse else range(count - 1)
    state = jnp.zeros(part.shape[:-1] + (DV,), jnp.float32)
    for index, source in enumerate(order):
        feed = gathered[source, ..., DK:].astype(jnp.float32)
        if index:
            moved = (
                jnp.matmul(
                    gathered[source, ..., :DK],
                    state.astype(jnp.bfloat16),
                    preferred_element_type=jnp.float32,
                )
                + feed
            )
        else:
            moved = feed
        ahead = source > place if reverse else source < place
        state = jnp.where(ahead, moved, state)
    return state


def rms_apply(values, gain):
    return values * lax.rsqrt(jnp.mean(values * values, axis=-1, keepdims=True) + EPSILON) * gain


def features(edged, mixer_in, conv_weight, decay_log):
    length = edged.shape[1] - (CONV - 1)
    taps = jnp.transpose(conv_weight, (2, 1, 0))[:, :, None, :]
    mixed = edged[:, 0:length] * taps[0]
    for index in range(1, CONV):
        mixed = mixed + edged[:, index : index + length] * taps[index]
    active = jax.nn.silu(mixed)
    query = active[..., :DK]
    key = active[..., DK : 2 * DK]
    value = active[..., 2 * DK :]
    query = (
        query * lax.rsqrt(jnp.sum(query * query, axis=-1, keepdims=True) + EPSILON) * DK ** (-0.5)
    )
    key = key * lax.rsqrt(jnp.sum(key * key, axis=-1, keepdims=True) + EPSILON)
    beta = jax.nn.sigmoid(mixer_in[0])
    logdecay = -jnp.exp(decay_log)[:, None] * jax.nn.softplus(mixer_in[1])
    return (query, key, value, beta, logdecay)


def fine(left, right):
    return jnp.matmul(left, right, precision=FINE)


def flip(array):
    return jnp.swapaxes(array, -1, -2)


@jax.custom_vjp
def unit_inverse(lower):
    width = lower.shape[-1]
    row_pos = lax.broadcasted_iota(jnp.int32, (width, width), 0)
    column = lax.broadcasted_iota(jnp.int32, (width, width), 1)

    def pairs(size):
        return (row_pos // size == column // size + 1) & ((row_pos // size) % 2 == 1)

    inverse = jnp.eye(width, dtype=lower.dtype) - jnp.where(pairs(1), lower, 0.0)
    size = 2
    while size < width:
        inverse = inverse - fine(fine(inverse, jnp.where(pairs(size), lower, 0.0)), inverse)
        size *= 2
    return inverse


def unit_inverse_fwd(lower):
    inverse = unit_inverse(lower)
    return inverse, inverse


def unit_inverse_bwd(inverse, grad):
    turned = flip(inverse)
    return (-fine(fine(turned, grad), turned),)


unit_inverse.defvjp(unit_inverse_fwd, unit_inverse_bwd)


def stretch_terms(query, key, value, beta, logdecay):
    width = query.shape[-2]
    row_pos = lax.broadcasted_iota(jnp.int32, (width, width), 0)
    column = lax.broadcasted_iota(jnp.int32, (width, width), 1)
    upto = (row_pos >= column).astype(jnp.float32)
    cumul = jnp.sum(upto * logdecay[..., None, :], axis=-1)
    last = jnp.sum(logdecay, axis=-1)[..., None, None]
    spread = cumul[..., :, None] - cumul[..., None, :]
    decay = jnp.exp(jnp.where(row_pos >= column, spread, NEGATIVE))
    strict = jnp.where(row_pos > column, decay, 0.0)
    lower = beta[..., None] * strict * fine(key, flip(key))
    inverse = unit_inverse(lower)
    growth = jnp.exp(cumul)[..., None]
    sides = jnp.concatenate(
        [(beta[..., None] * growth) * key, beta[..., None] * value], axis=-1
    )
    solved = jnp.matmul(inverse, sides)
    scores = decay * jnp.matmul(query, flip(key))
    mapped = jnp.matmul(scores, solved)
    query_map = growth * query - mapped[..., :DK]
    out_fixed = mapped[..., DK:]
    key_end = jnp.exp(last - cumul[..., None]) * key
    ended = jnp.matmul(flip(key_end), solved)
    transit = jnp.exp(last) * jnp.eye(DK, dtype=query.dtype) - ended[..., :DK]
    feed = ended[..., DK:]
    return (query_map, out_fixed, transit, feed)


def gated(layer_outputs, gate, gain):
    return rms_apply(layer_outputs, gain) * jax.nn.silu(gate)


def swiglu(gate_up):
    return jax.nn.silu(gate_up[:, 0]) * gate_up[:, 1]


def chain(maps, feeds):
    start = jnp.concatenate(
        [
            jnp.broadcast_to(jnp.eye(DK, dtype=jnp.float32), maps[0].shape),
            jnp.zeros_like(feeds[0]),
        ],
        axis=-1,
    )
    pad = ((0, 0), (0, 0), (DK, 0))
    states = [start]
    for index, (part, feed) in enumerate(zip(maps, feeds)):
        if index == 0:
            states.append(jnp.concatenate([part, feed], axis=-1))
        else:
            states.append(fine(part, states[-1]) + jnp.pad(feed, pad))
    return states


def shards(
    block_input,
    norm1_gain,
    w_in,
    w_ba,
    conv_weight,
    decay_log,
    gnorm_gain,
    w_out,
    norm2_gain,
    w_up,
    w_down,
    grad_out,
):
    length = block_input.shape[0]
    heads = w_in.shape[1]
    channels = conv_weight.shape[0]
    blocks = length // STRETCH
    f32 = jnp.float32
    bf16 = jnp.bfloat16

    def split(array):
        return array.reshape((heads, blocks, STRETCH) + array.shape[2:])

    tokens_wide = block_input.astype(f32)
    normed, pull_first = jax.vjp(rms_apply, tokens_wide, norm1_gain)
    normed_b = normed.astype(bf16)
    projected = jnp.einsum(
        "td,dhc->htc", normed_b, w_in, preferred_element_type=f32
    ).astype(bf16)
    mixer_in = jnp.einsum("td,dch->cht", normed_b, w_ba, preferred_element_type=f32)
    edge = shifted(projected[:, length - (CONV - 1) :, :channels], "seq", 1)
    edged = jnp.concatenate([edge, projected[:, :, :channels]], 1).astype(f32)
    feats, pull_feat = jax.vjp(features, edged, mixer_in, conv_weight, decay_log)
    terms, pull_terms = jax.vjp(stretch_terms, *[split(a) for a in feats])
    query_map, out_fixed, transit, feed = terms
    starts = chain(
        [transit[:, i] for i in range(blocks)], [feed[:, i] for i in range(blocks)]
    )
    carried = carried_states(starts[-1], False)
    before = jnp.stack(starts[:-1], axis=1)
    states = jnp.matmul(before[..., :DK], carried[:, None]) + before[..., DK:]
    layer_outputs = (jnp.matmul(query_map, states) + out_fixed).reshape(heads, length, DV)
    gate_wide = projected[:, :, channels:].astype(f32)
    gated_out, pull_gate = jax.vjp(gated, layer_outputs, gate_wide, gnorm_gain)
    gated_b = gated_out.astype(bf16)
    mixer_part = jnp.einsum("htc,chd->td", gated_b, w_out, preferred_element_type=f32)
    mixed = head_sum(mixer_part).astype(f32)
    hidden = tokens_wide + mixed
    hidden_n, pull_second = jax.vjp(rms_apply, hidden, norm2_gain)
    hidden_b = hidden_n.astype(bf16)
    gate_up = jnp.einsum("td,dcf->tcf", hidden_b, w_up, preferred_element_type=f32)
    swish, pull_swish = jax.vjp(swiglu, gate_up)
    swish_b = swish.astype(bf16)
    act_grad = jnp.dot(grad_out, w_down, preferred_element_type=f32)
    (gate_up_grad,) = pull_swish(act_grad)
    gate_up_b = gate_up_grad.astype(bf16)
    second_part = jnp.einsum("tcf,dcf->td", gate_up_b, w_up, preferred_element_type=f32)
    second_total = head_sum(second_part).astype(f32)
    down_grad = lax.dot_general(
        grad_out, swish_b, (((0,), (0,)), ((), ())), preferred_element_type=f32
    )
    up_grad = jnp.einsum("td,tcf->dcf", hidden_b, gate_up_b, preferred_element_type=f32)
    up_share = seq_share(up_grad)
    down_share = seq_share(down_grad)
    hidden_grad, gain_second = pull_second(second_total)
    stream = grad_out.astype(f32) + hidden_grad
    stream_b = stream.astype(bf16)
    gated_grad = jnp.einsum("td,chd->htc", stream_b, w_out, preferred_element_type=f32)
    output_gradient, gate_grad, gain_gated = pull_gate(gated_grad)
    out_weight_grad = jnp.einsum("htc,td->chd", gated_b, stream_b, preferred_element_type=f32)
    out_share = seq_share(out_weight_grad)
    out_split = split(output_gradient)
    back_feed = jnp.matmul(flip(query_map), out_split)
    turned = flip(transit)
    backs = chain(
        [turned[:, i] for i in reversed(range(blocks))],
        [back_feed[:, i] for i in reversed(range(blocks))],
    )
    later_grad = carried_states(backs[-1], True)
    after = jnp.stack(backs[:-1][::-1], axis=1)
    later = jnp.matmul(after[..., :DK], later_grad[:, None]) + after[..., DK:]
    term_grad = (
        jnp.matmul(out_split, flip(states)),
        out_split,
        jnp.matmul(later, flip(states)),
        later,
    )
    feat_grad = [
        a.reshape((heads, length) + a.shape[3:]) for a in pull_terms(term_grad)
    ]
    edged_grad, mixer_grad, conv_grad, log_decay_gradient = pull_feat(tuple(feat_grad))
    back_edge = shifted(edged_grad[:, : CONV - 1], "seq", -1)
    channel_grad = edged_grad[:, CONV - 1 :]
    channel_grad = jnp.concatenate(
        [
            channel_grad[:, : length - (CONV - 1)],
            channel_grad[:, length - (CONV - 1) :] + back_edge,
        ],
        1,
    )
    proj_grad = jnp.concatenate([channel_grad, gate_grad], 2).astype(bf16)
    mixer_b = mixer_grad.astype(bf16)
    first_part = jnp.einsum("htc,dhc->td", proj_grad, w_in, preferred_element_type=f32)
    first_part = first_part + jnp.einsum(
        "cht,dch->td", mixer_b, w_ba, preferred_element_type=f32
    )
    first_total = head_sum(first_part).astype(f32)
    ffn_part = lax.dot_general(
        swish_b, w_down, (((1,), (1,)), ((), ())), preferred_element_type=f32
    )
    result = hidden + head_sum(ffn_part).astype(f32)
    in_weight_grad = jnp.einsum("td,htc->dhc", normed_b, proj_grad, preferred_element_type=f32)
    in_share = seq_share(in_weight_grad)
    gate_weight_grad = jnp.einsum("td,cht->dch", normed_b, mixer_b, preferred_element_type=f32)
    input_part, gain_first = pull_first(first_total)
    input_grad = stream + input_part
    small = [
        gain_first,
        gain_second,
        lax.psum(gain_gated, "head"),
        log_decay_gradient,
        conv_grad.reshape(-1),
        gate_weight_grad.reshape(-1),
    ]
    summed = lax.psum(jnp.concatenate(small), "seq")
    pieces, at = [], 0
    for part in small:
        pieces.append(summed[at : at + part.shape[0]])
        at += part.shape[0]
    gain_one, gain_two, gain_norm, decay_total, conv_total, gate_total = pieces
    count = lax.axis_size("seq")
    place = lax.axis_index("seq")

    def mine(flat, shape):
        share = flat.shape[0] // count
        piece = lax.dynamic_slice(flat, (place * share,), (share,))
        return piece.reshape((shape[0] // count,) + shape[1:])

    return (
        result,
        input_grad,
        gain_one,
        in_share,
        mine(gate_total, gate_weight_grad.shape),
        mine(conv_total, conv_grad.shape),
        decay_total,
        gain_norm,
        out_share,
        gain_two,
        up_share,
        down_share,
    )


def solution(mesh):
    return jax.shard_map(
        shards,
        mesh=mesh,
        in_specs=(
            P("seq", None),
            P(),
            P(None, "head", None),
            P(None, None, "head"),
            P(None, "head", None),
            P("head"),
            P(),
            P(None, "head", None),
            P(),
            P(None, None, "head"),
            P(None, "head"),
            P("seq", None),
        ),
        out_specs=(
            P("seq", None),
            P("seq", None),
            P(),
            P("seq", "head", None),
            P("seq", None, "head"),
            P("seq", "head", None),
            P("head"),
            P(),
            P("seq", "head", None),
            P(),
            P("seq", None, "head"),
            P("seq", "head"),
        ),
        check_vma=False,
    )
```

time: 1190 us -> 636 us (0.53)
  waiting for transfers between devices: 701 us -> 343 us
  matrix products: 218 us -> 103 us
  other arithmetic: 130 us -> 48.5 us
  local copies, waits for them, and re-layouts: 81.8 us -> 62.5 us
  blocking collectives: 29.5 us -> 44.3 us
    reduce_scatter x3 -> x1, waiting for transfers between devices: 279 us -> 75.2 us  [seq_share(): lax.psum_scatter(grad.astype(jnp.bfloat16), 'seq', scatter_dimension=0, t...]
    all_gather x4 -> x2, waiting for transfers between devices: 159 us -> 53.4 us  [carried_states(): gathered = lax.all_gather(part.astype(jnp.bfloat16), 'seq')]
    dot_general x113 -> x70, matrix products: 202 us -> 96.9 us  [the longest x27 15.1 us: fine(): return jnp.matmul(left, right, precision=FINE)]
    another operation x8 -> x1, other arithmetic: 84.4 us -> 0.02 us  [the longest x5 82 us: stretch_terms(): jax.scipy.linalg.solve_triangular(system, (beta * jnp.exp(cumul))[:, None...]
    psum x4 -> x3, waiting for transfers between devices: 179 us -> 111 us  [head_sum(): return lax.psum(part.astype(jnp.bfloat16), 'head')]
    dynamic_update_slice x24 -> x0, local copies, waits for them, and re-layouts: 24.1 us -> none  [scan_head(): final, layer_outputs = lax.scan(scan_advance, state, terms)]
    unnamed x17 -> x12, waiting for transfers between devices: 83.7 us -> 103 us
    psum x2, blocking collectives: 29.5 us -> 44.3 us  [the longest x1 38.3 us: shards(): summed = lax.psum(jnp.concatenate(small), 'seq')]
  transfers between devices with their start and end apart: 16 -> 11, of which waited for: 13 -> 9; matrix products, arithmetic and copies ran while one was open for 19% -> 19% of each run, Pallas kernels for 0% -> 0%
where the time goes in v1:
time: 636 us; the launch traced here: 625 us
  waiting for transfers between devices  343 us (54%)
  matrix products  103 us (16%)
  local copies, waits for them, and re-layouts  62.5 us (10%)
  other arithmetic  48.5 us (8%)
  blocking collectives  44.3 us (7%)
  between operations  16.9 us (3%)
  starting transfers between devices  7.44 us (1%)
    psum x3, waiting for transfers between devices, head_sum(): return lax.psum(part.astype(jnp.bfloat16), 'head')  111 us
    unnamed x12, waiting for transfers between devices  103 us
    reduce_scatter x1, waiting for transfers between devices, seq_share(): lax.psum_scatter(grad.astype(jnp.bfloat16), 'seq', scatter_dimension=0, t...  75.2 us
    all_gather x2, waiting for transfers between devices, carried_states(): gathered = lax.all_gather(part.astype(jnp.bfloat16), 'seq')  53.4 us
    unnamed x304, local copies, waits for them, and re-layouts  42.4 us
    psum x1, blocking collectives, shards(): summed = lax.psum(jnp.concatenate(small), 'seq')  38.3 us
    dot_general x27, matrix products, fine(): return jnp.matmul(left, right, precision=FINE)  15.1 us
  transfers between devices with their start and end apart: 11, of which 9 were waited for; matrix products, arithmetic and copies ran while one was open for 19% of the time, Pallas kernels for 0%

profile of v1, /device:TPU:0, one launch (start us, length us, event | category | flops | bytes accessed | tf_op | source)
XLA Modules:
  0.0 625.0 jit_solution(16080027719783701576)
XLA Ops:
  12.8 5.0 collective-permute-start
  56.8 38.7 %all-gather.5.cloned.1.call-done = bf16[16,128,384]{2,1,0:T(8,128)(2,1)} async-done(((bf16[2,128,384]{2,1,0:T(8,128)(2,1)}), bf16[16,128,384]{2,1,0:T(8,128)(2,1)}) %all-gather.5.cloned.1.call-update) | async-done | bytes 1572880 | tf_op jit(solution)/shard_map/all_gather | solution.py:36
  101.3 3.6 slice_add_fusion.1
  112.6 34.8 %all-reduce.41.cloned.1.call-done = bf16[512,1024]{1,0:T(8,128)(2,1)} async-done(((bf16[512,1024]{1,0:T(8,128)(2,1)}), bf16[512,1024]{1,0:T(8,128)(2,1)}) %all-reduce.41.cloned.1.call-update) | async-done | bytes 1048592 | tf_op jit(solution)/shard_map/psum | solution.py:24
  149.5 3.8 fusion.252
  163.8 33.3 %all-reduce.43.cloned.1.call-done = bf16[512,1024]{1,0:T(8,128)(2,1)} async-done(((bf16[512,1024]{1,0:T(8,128)(2,1)}), bf16[512,1024]{1,0:T(8,128)(2,1)}) %all-reduce.43.cloned.1.call-update) | async-done | bytes 1048592 | tf_op jit(solution)/shard_map/psum | solution.py:24
  200.7 4.2 multiply_reduce_fusion.5
  215.5 4.5 fusion.42
  220.0 3.7 copy.348
  234.7 3.6 multiply_reduce_fusion.12
  245.6 14.8 %all-gather.7.cloned.1.call-done = bf16[16,128,384]{2,1,0:T(8,128)(2,1)} async-done(((bf16[2,128,384]{2,1,0:T(8,128)(2,1)}), bf16[16,128,384]{2,1,0:T(8,128)(2,1)}) %all-gather.7.cloned.1.call-update) | async-done | bytes 1572880 | tf_op jit(solution)/shard_map/all_gather | solution.py:36
  266.2 4.2 slice_add_fusion
  296.6 4.8 pad_add_fusion.1
  307.0 5.8 convolution_convert_fusion.1
  312.8 4.6 copy.381
  318.0 5.3 convolution_convert_fusion
  325.2 6.1 psum.46
  331.3 9.2 %all-reduce.45.cloned.1.call-done = bf16[256,2,1024]{2,1,0:T(2,128)(2,1)} async-done(((bf16[256,2,1024]{2,1,0:T(2,128)(2,1)}), bf16[256,2,1024]{2,1,0:T(2,128)(2,1)}) %all-reduce.45.cloned.1.call-update) | async-done | bytes 1048592
  342.2 66.7 %reduce-scatter.12.cloned.1.call-done = bf16[128,704]{1,0:T(8,128)(2,1)} async-done(((bf16[1024,704]{1,0:T(8,128)(2,1)}), bf16[128,704]{1,0:T(8,128)(2,1)}) %reduce-scatter.12.cloned.1.call-update) | async-done | bytes 180240
  418.9 43.3 %all-reduce.47.cloned.1.call-done = (bf16[512,1024]{1,0:T(8,128)(2,1)}, bf16[512,1024]{1,0:T(8,128)(2,1)}) async-done(((bf16[512,1024]{1,0:T(8,128)(2,1)}, bf16[512,1024]{1,0:T(8,128)(2,1)}), (bf16[512,1024]{1,0:T(8,128)(2,1)}, bf16[512,1024]{1,0:T(8,128)(2,1)})) %all-reduce.47.cloned.1.call-update) | async-done | bytes 2097168 | tf_op jit(solution)/shard_map/psum | solution.py:24
  464.7 38.3 %psum.47 = f32[10498]{0:T(1024)S(1)} all-reduce(f32[10498]{0:T(1024)S(1)} %concatenate.34), channel_id=1, replica_groups=mesh['seq'=8,'head'=4] {'seq'}, use_global_device_ids=true, to_apply=%region_35.36 | all-reduce | flops 10498 | bytes 83984 | tf_op jit(solution)/shard_map/psum | solution.py:297
  506.7 5.0 fusion.19
  511.7 26.9 %reduce-scatter.10.cloned.1.call-done = bf16[128,1408]{1,0:T(8,128)(2,1)} async-done(((bf16[1024,1408]{1,0:T(8,128)(2,1)}), bf16[128,1408]{1,0:T(8,128)(2,1)}) %reduce-scatter.10.cloned.1.call-update) | async-done | bytes 360464
  540.7 75.2 %reduce-scatter.8.cloned.1.call-done = bf16[128,2,768]{2,0,1:T(8,128)(2,1)} async-done(((bf16[1024,2,768]{2,0,1:T(8,128)(2,1)}), bf16[128,2,768]{2,0,1:T(8,128)(2,1)}) %reduce-scatter.8.cloned.1.call-update) | async-done | bytes 393232 | tf_op jit(solution)/shard_map/reduce_scatter | solution.py:28
  (492 shorter events, 163.0 us)
Async XLA Ops:
  7.2 88.3 %all-gather.5.cloned.1.call-start = ((), (), s32[]{:S(2)}) async-start(), calls=%async_computation.6 | async-start | bytes 1769472 | tf_op jit(solution)/shard_map/all_gather | solution.py:36
  12.8 15.5 %collective-permute-start = (bf16[2,3,512]{2,1,0:T(4,128)(2,1)S(1)}, bf16[2,3,512]{2,1,0:T(4,128)(2,1)S(1)}, u32[]{:S(2)}, u32[]{:S(2)}) collective-permute-start(bf16[2,3,512]{2,1,0:T(4,128)(2,1)S(1)} %slice.386), channel_id=1, source_target_pairs={{0,4},{4,8},{8,12},{12,16},{16,20},{20,24},{24,28},{1,5},{5,9},{9,... | collective-permute-start | bytes 18440 | tf_op jit(solution)/shard_map/ppermute | solution.py:20
  17.8 10.4 %copy-start.79 = (f32[64,64]{1,0:T(8,128)}, f32[64,64]{1,0:T(8,128)S(1)}, u32[]{:S(2)}) copy-start(f32[64,64]{1,0:T(8,128)S(1)} %fusion.212) | copy-start | bytes 49156
  18.5 20.5 %copy-start.75 = (pred[64,64]{1,0:T(8,128)(4,1)}, pred[64,64]{1,0:T(8,128)(4,1)S(1)}, u32[]{:S(2)}) copy-start(pred[64,64]{1,0:T(8,128)(4,1)S(1)} %iota_compare_fusion.2) | copy-start | bytes 12292
  18.6 142.0 %copy-start.60 = (f32[128,128]{1,0:T(8,128)}, f32[128,128]{1,0:T(8,128)S(1)}, u32[]{:S(2)}) copy-start(f32[128,128]{1,0:T(8,128)S(1)} %fusion.189) | copy-start | bytes 196612
  20.0 19.1 %copy-start.62 = (f32[2,8,64]{2,1,0:T(8,128)}, f32[2,8,64]{2,1,0:T(8,128)S(1)}, u32[]{:S(2)}) copy-start(f32[2,8,64]{2,1,0:T(8,128)S(1)} %div.147) | copy-start | bytes 12292
  20.0 9.9 %copy-start.66 = (f32[2,128,128]{2,1,0:T(8,128)}, f32[2,128,128]{2,1,0:T(8,128)S(1)}, u32[]{:S(2)}) copy-start(f32[2,128,128]{2,1,0:T(8,128)S(1)} %broadcast_in_dim.108) | copy-start | bytes 393220
  21.8 19.1 %copy-start.81 = (f32[2,8,64]{2,1,0:T(8,128)}, f32[2,8,64]{2,1,0:T(8,128)S(1)}, u32[]{:S(2)}) copy-start(f32[2,8,64]{2,1,0:T(8,128)S(1)} %get-tuple-element.163) | copy-start | bytes 12292
  21.8 186.0 %copy-start.83 = (f32[2,8,64]{2,1,0:T(8,128)}, f32[2,8,64]{2,1,0:T(8,128)S(1)}, u32[]{:S(2)}) copy-start(f32[2,8,64]{2,1,0:T(8,128)S(1)} %get-tuple-element.161) | copy-start | bytes 12292
  32.8 18.1 %copy-start.99 = (f32[2,512]{1,0:T(2,128)}, f32[2,512]{1,0:T(2,128)S(1)}, u32[]{:S(2)}) copy-start(f32[2,512]{1,0:T(2,128)S(1)} %get-tuple-element.96) | copy-start | bytes 12292
  50.8 96.5 %all-reduce.41.cloned.1.call-start = ((), (), s32[]{:S(2)}) async-start(), calls=%async_computation.3 | async-start | bytes 2097152 | tf_op jit(solution)/shard_map/psum | solution.py:24
  112.5 37.0 %copy-start.119 = (f32[1024]{0:T(1024)S(1)}, f32[1024]{0:T(1024)}, u32[]{:S(2)}) copy-start(f32[1024]{0:T(1024)} %param.20) | copy-start | bytes 12292
  112.5 84.6 %all-reduce.43.cloned.1.call-start = ((), (), s32[]{:S(2)}) async-start(), calls=%async_computation.4 | async-start | bytes 2097152 | tf_op jit(solution)/shard_map/psum | solution.py:24
  149.5 51.1 %copy-start.109 = (f32[512]{0:T(512)}, f32[512]{0:T(512)S(1)}, u32[]{:S(2)}) copy-start(f32[512]{0:T(512)S(1)} %fusion.222) | copy-start | bytes 6148
  160.2 100.2 %all-gather.7.cloned.1.call-start = ((), (), s32[]{:S(2)}) async-start(), calls=%async_computation.7 | async-start | bytes 1769472 | tf_op jit(solution)/shard_map/all_gather | solution.py:36
  215.4 125.0 %all-reduce.45.cloned.1.call-start = ((), (), s32[]{:S(2)}) async-start(), calls=%async_computation.10 | async-start | bytes 2097152
  223.7 185.1 %reduce-scatter.12.cloned.1.call-start = ((), (), s32[]{:S(2)}) async-start(), calls=%async_computation.9 | async-start | bytes 1769472
  234.5 227.7 %all-reduce.47.cloned.1.call-start = ((), (), s32[]{:S(2)}) async-start(), calls=%async_computation.11 | async-start | bytes 4194304 | tf_op jit(solution)/shard_map/psum | solution.py:24
  292.9 8.7 %collective-permute-start.1 = (f32[2,3,512]{2,1,0:T(4,128)S(1)}, f32[2,3,512]{2,1,0:T(4,128)S(1)}, u32[]{:S(2)}, u32[]{:S(2)}) collective-permute-start(f32[2,3,512]{2,1,0:T(4,128)S(1)} %pad_add_fusion.5), channel_id=1, source_target_pairs={{4,0},{8,4},{12,8},{16,12},{20,16},{24,20},{28,24},{5,1},{9,5},{13... | collective-permute-start | bytes 36872 | tf_op jit(solution)/shard_map/ppermute | solution.py:20
  306.9 231.6 %reduce-scatter.10.cloned.1.call-start = ((), (), s32[]{:S(2)}) async-start(), calls=%async_computation.8 | async-start | bytes 3244032
  317.4 298.5 %reduce-scatter.8.cloned.1.call-start = ((), (), s32[]{:S(2)}) async-start(), calls=%async_computation.5 | async-start | bytes 3538944 | tf_op jit(solution)/shard_map/reduce_scatter | solution.py:28
  413.6 51.0 %copy-start.121 = (f32[1024]{0:T(1024)S(1)}, f32[1024]{0:T(1024)}, u32[]{:S(2)}) copy-start(f32[1024]{0:T(1024)} %get-tuple-element.90) | copy-start | bytes 12292
  416.1 89.9 %copy-start.112 = (f32[512]{0:T(512)S(1)}, f32[512]{0:T(512)}, u32[]{:S(2)}) copy-start(f32[512]{0:T(512)} %copy-done.111) | copy-start | bytes 6148
  416.1 90.5 %copy-start.128 = (f32[512]{0:T(512)S(1)}, f32[512]{0:T(512)}, u32[]{:S(2)}) copy-start(f32[512]{0:T(512)} %copy-done.127) | copy-start | bytes 6148
  (131 other events, 413.4 us)
Sparse Core Ops, SparseCore 0:
  51.0 44.4 all-gather.4
  112.7 34.6 all-reduce.40
  160.3 36.7 all-reduce.42
  215.6 44.7 all-gather.6
  263.7 76.6 all-reduce.44
  343.7 65.0 reduce-scatter.11
  411.9 50.2 all-reduce.46
  465.7 72.8 reduce-scatter.9
  542.1 73.6 reduce-scatter.7
